TPU v7x, 32 devices: a whole 2x2x4 slice. The times are simulated.
32 devices in a mesh: video: 2 (over x), row: 16 (over z, y, core).
Axes of the slice: x: 2, y: 2, z: 4, core: 2. Of those that a mesh axis runs over, the one named last changes fastest.
Arguments:
- stream: bfloat16 [8, 16, 32, 1536], P('video', 'row'), parts along dimension 0, may hold values from -0.8984375 to 0.8984375
- query: bfloat16 [8, 16, 32, 1536], P('video', 'row'), parts along dimension 0, may hold values from -30 to 30
- key: bfloat16 [8, 16, 32, 1536], P('video', 'row'), parts along dimension 0, may hold values from -6 to 6
- value: bfloat16 [8, 16, 32, 1536], P('video', 'row'), parts along dimension 0, may hold values from -6 to 6
- attn_gate: float32 [3072], P('video'), parts along dimension 0, may hold values from 1 to 3
- shift_mod: float32 [3072], P('video'), parts along dimension 0, may hold values from -3 to 3
- scale_mod: float32 [3072], P('video'), parts along dimension 0, may hold values from -3 to 3
- head_weight: bfloat16 [1536, 64], replicated, may hold values from -0.15625 to 0.15625
- head_bias: float32 [64], replicated, may hold values from -3 to 3
- latent_mean: float32 [16], replicated, may hold values from -3 to 3
- latent_std: float32 [16], replicated, may hold values from 0.5 to 2
- conv_in_weight: bfloat16 [3, 3, 3, 16, 384], replicated, may hold values from -0.3125 to 0.3125
- conv_in_bias: float32 [384], replicated, may hold values from -2 to 2
- norm_gain: float32 [384], replicated, may hold values from 0.5 to 1.5
- conv_weight: bfloat16 [3, 3, 3, 384, 384], replicated, may hold values from -0.0625 to 0.0625
- conv_bias: float32 [384], replicated, may hold values from -2 to 2
Outputs:
- decoded: bfloat16 [8, 32, 64, 384], P('video', 'row'), parts along dimension 0
There are 2 independent parts, one for each index of `video`. A program takes and returns all parts, laid end to end along the dimension named above; an argument that names none is the same for every part. Nothing has to cross between parts.
All inputs are finite; a program needn't handle non-finite values.
Results may differ from a plain program's by a relative error of at most 0.0069.
Values may be sent and summed in bfloat16 or wider, within the bound.
A program may use at most 128 MiB of HBM per device.

v0:
```python
import math

import jax
import jax.numpy as jnp
import numpy as np
from jax import lax
from jax.sharding import PartitionSpec as P

HEADS = 12
LAT = 16


def shifted(block, axis, distance):
    devices = range(lax.axis_size(axis))
    route = [(i - distance, i) for i in devices if i - distance in devices]
    return lax.ppermute(block, axis, route)


def with_halo(cells, sides, width):
    for axis, dim in sides:
        count = lax.axis_size(axis)
        ends = count - 1
        head = lax.slice_in_dim(cells, 0, width, axis=dim)
        tail = lax.slice_in_dim(cells, cells.shape[dim] - width, cells.shape[dim], axis=dim)
        cells = jnp.concatenate(
            [
                lax.ppermute(tail, axis, [(i, (i + 1) % count) for i in range(ends)]),
                cells,
                lax.ppermute(head, axis, [((i + 1) % count, i) for i in range(ends)]),
            ],
            axis=dim,
        )
    return cells


def causal_conv(rows_padded, weight):
    frames, padded_rows, columns, in_width = rows_padded.shape
    out_rows = padded_rows - 2
    out_width = weight.shape[-1]
    padded = jnp.pad(rows_padded, ((2, 0), (0, 0), (1, 1), (0, 0)))
    summed = jnp.zeros((frames * out_rows * columns, out_width), jnp.float32)
    for a in range(3):
        pieces = [
            padded[a : a + frames, b : b + out_rows, e : e + columns]
            for b in range(3)
            for e in range(3)
        ]
        stacked_taps = jnp.concatenate(pieces, axis=-1).reshape(-1, 9 * in_width)
        summed = summed + jnp.dot(
            stacked_taps,
            weight[a].reshape(9 * in_width, out_width),
            preferred_element_type=jnp.float32,
        )
    return summed.reshape(frames, out_rows, columns, out_width)


def activate(hidden, gain):
    values = hidden.astype(jnp.float32)
    scaled = values * lax.rsqrt(jnp.mean(values * values, axis=-1, keepdims=True) + 1e-06) * gain
    return jax.nn.silu(scaled).astype(jnp.bfloat16)


def shards(
    stream,
    query,
    key,
    value,
    attn_gate,
    shift_mod,
    scale_mod,
    head_weight,
    head_bias,
    latent_mean,
    latent_std,
    conv_in_weight,
    conv_in_bias,
    norm_gain,
    conv_weight,
    conv_bias,
):
    frames, own_rows, columns, width = query.shape
    head_size = width // HEADS
    scaling = head_size ** (-0.5)
    paired = jnp.stack([key, value], axis=0)
    reach = (own_rows + 2) // own_rows
    above = []
    below = []
    for j in range(1, reach + 1):
        above.insert(0, shifted(paired, "row", j))
        below.append(shifted(paired, "row", -j))
    extended = jnp.concatenate(above + [paired] + below, axis=2)
    tile_size = math.gcd(columns, 16)
    tile_count = columns // tile_size
    span_width = min(tile_size + 6, columns)
    tile_first = np.arange(tile_count) * tile_size
    key_start = np.minimum(np.clip(tile_first - 3, 0, columns - 7), columns - span_width)
    key_cols = key_start[:, None] + np.arange(span_width)[None, :]
    col_start = np.clip(np.arange(columns) - 3, 0, columns - 7).reshape(tile_count, tile_size)
    band = jnp.asarray(
        (key_cols[:, None, :] >= col_start[:, :, None])
        & (key_cols[:, None, :] < col_start[:, :, None] + 7)
    )
    tiled_pair = extended[:, :, :, key_cols.reshape(-1)].reshape(
        2, frames, own_rows + 6, tile_count, span_width, HEADS, head_size
    )
    keys_ext = tiled_pair[0]
    values_ext = tiled_pair[1]
    queries = query.reshape(frames, own_rows, tile_count, tile_size, HEADS, head_size)
    frame_start = np.clip(np.arange(frames) - 1, 0, frames - 3)
    first_row = lax.axis_index("row") * own_rows + jnp.arange(own_rows, dtype=jnp.int32)
    all_rows = own_rows * lax.axis_size("row")
    scores = []
    value_blocks = []
    for a in range(3):
        key_frames = keys_ext[frame_start + a]
        value_frames = values_ext[frame_start + a]
        for r in range(7):
            key_block = key_frames[:, r : r + own_rows]
            value_blocks.append(value_frames[:, r : r + own_rows])
            raw = (
                jnp.einsum(
                    "finwhd,finvhd->finwhv", queries, key_block, preferred_element_type=jnp.float32
                )
                * scaling
            )
            source_row = first_row + (r - 3)
            row_valid = (source_row >= 0) & (source_row < all_rows)
            allowed = row_valid[None, :, None, None, None, None] & band[None, None, :, :, None, :]
            scores.append(jnp.where(allowed, raw, -jnp.inf))
    peak = jnp.max(scores[0], axis=5, keepdims=True)
    for index in range(1, 21):
        peak = jnp.maximum(peak, jnp.max(scores[index], axis=5, keepdims=True))
    total = jnp.zeros(peak.shape, jnp.float32)
    for index in range(21):
        total = total + jnp.sum(jnp.exp(scores[index] - peak), axis=5, keepdims=True)
    attended = jnp.zeros((frames, own_rows, tile_count, tile_size, HEADS, head_size), jnp.float32)
    for index in range(21):
        block_probs = (jnp.exp(scores[index] - peak) / total).astype(jnp.bfloat16)
        attended = attended + jnp.einsum(
            "finwhv,finvhd->finwhd",
            block_probs,
            value_blocks[index],
            preferred_element_type=jnp.float32,
        )
    attn = attended.reshape(frames, own_rows, columns, width).astype(jnp.bfloat16)
    attn = lax.optimization_barrier(attn)
    resid = stream.astype(jnp.float32) + attn_gate * attn.astype(jnp.float32)
    center = resid - jnp.mean(resid, axis=-1, keepdims=True)
    spread = jnp.mean(center * center, axis=-1, keepdims=True)
    normed = (center * lax.rsqrt(spread + 1e-06) * (1.0 + scale_mod) + shift_mod).astype(
        jnp.bfloat16
    )
    patch = (
        jnp.dot(normed.reshape(-1, width), head_weight, preferred_element_type=jnp.float32)
        + head_bias
    )
    patch = (
        patch.reshape(frames, own_rows, columns, 2, 2, LAT)
        .transpose(0, 1, 3, 2, 4, 5)
        .reshape(frames, 2 * own_rows, 2 * columns, LAT)
    )
    latent = (patch * latent_std + latent_mean).astype(jnp.bfloat16)
    edge = with_halo(latent, (("row", 1),), 1)
    hidden = (causal_conv(edge, conv_in_weight) + conv_in_bias).astype(jnp.bfloat16)
    hidden = lax.optimization_barrier(hidden)
    edge_act = with_halo(activate(hidden, norm_gain), (("row", 1),), 1)
    mixed = causal_conv(edge_act, conv_weight)
    return (hidden.astype(jnp.float32) + mixed + conv_bias).astype(jnp.bfloat16)


def solution(mesh):
    return jax.shard_map(
        shards,
        mesh=mesh,
        in_specs=(
            P("video", "row", None, None),
            P("video", "row", None, None),
            P("video", "row", None, None),
            P("video", "row", None, None),
            P("video"),
            P("video"),
            P("video"),
            P(),
            P(),
            P(),
            P(),
            P(),
            P(),
            P(),
            P(),
            P(),
        ),
        out_specs=P("video", "row", None, None),
        check_vma=False,
    )
```

profile of v0, /device:TPU:1, one launch (start us, length us, event | category | flops | bytes accessed | tf_op | source)
XLA Modules:
  0.0 315.4 jit_solution(3203584440973379253)
XLA Ops:
  0.1 1.8 copy_bitcast_fusion.84
  2.4 5.5 %collective-permute-start = (bf16[2,4,1,32,1536]{4,1,3,2,0:T(4,128)(2,1)S(1)}, bf16[2,4,1,32,1536]{4,1,3,2,0:T(4,128)(2,1)}, u32[]{:S(2)}, u32[]{:S(2)}) collective-permute-start(bf16[2,4,1,32,1536]{4,1,3,2,0:T(4,128)(2,1)S(1)} %pad_maximum_fusion), channel_id=1, source_target_pairs={{0,3},{1,4},{2,5},{3,6},{4,7},{5,8},{6,9},{7,10},{8,11},{9,12},{10... | collective-permute-start | bytes 2359304 | tf_op jit(solution)/shard_map/ppermute | solution.py:16
  7.9 3.2 collective-permute-start.1
  11.0 2.2 collective-permute-start.2
  13.3 3.0 collective-permute-start.3
  16.3 1.3 collective-permute-start.4
  17.6 1.3 reshape.817
  19.2 1.3 collective-permute-start.5
  20.5 2.3 constant_dynamic-update-slice_fusion.6
  22.8 38.5 %collective-permute-done.1 = bf16[2,4,1,32,1536]{4,1,3,2,0:T(4,128)(2,1)} collective-permute-done((bf16[2,4,1,32,1536]{4,1,3,2,0:T(4,128)(2,1)S(1)}, bf16[2,4,1,32,1536]{4,1,3,2,0:T(4,128)(2,1)}, u32[]{:S(2)}, u32[]{:S(2)}) %collective-permute-start.1) | collective-permute-done | bytes 786464 | tf_op jit(solution)/shard_map/ppermute | solution.py:16
  61.3 2.3 constant_dynamic-update-slice_fusion.5
  63.6 11.2 %collective-permute-done.2 = bf16[2,4,1,32,1536]{4,1,3,2,0:T(4,128)(2,1)} collective-permute-done((bf16[2,4,1,32,1536]{4,1,3,2,0:T(4,128)(2,1)S(1)}, bf16[2,4,1,32,1536]{4,1,3,2,0:T(4,128)(2,1)}, u32[]{:S(2)}, u32[]{:S(2)}) %collective-permute-start.2) | collective-permute-done | bytes 786464 | tf_op jit(solution)/shard_map/ppermute | solution.py:16
  74.9 2.3 constant_dynamic-update-slice_fusion.4
  77.2 1.2 constant_dynamic-update-slice_fusion.3
  78.4 2.3 constant_dynamic-update-slice_fusion.2
  80.7 1.2 constant_dynamic-update-slice_fusion.1
  81.9 1.2 constant_dynamic-update-slice_fusion
  83.1 12.2 %gather_fusion = bf16[44,2,4,7,1536]{4,2,3,1,0:T(4,128)(2,1)} fusion(bf16[2,4,7,32,1536]{4,1,3,2,0:T(4,128)(2,1)} %constant_dynamic-update-slice_fusion, s32[1024]{0:T(1024)S(1)} %pad_clamp_fusion.3), kind=kCustom, calls=%fused_computation | custom fusion | bytes 15138992 | tf_op jit(solution)/shard_map/gather | solution.py:103
  95.3 7.6 %fusion.148 = (bf16[1,4,7,44,1536]{4,1,2,0,3:T(4,128)(2,1)}, bf16[1,4,7,44,1536]{4,1,2,0,3:T(4,128)(2,1)}) fusion(bf16[2,4,7,44,1536]{4,1,2,0,3:T(4,128)(2,1)} %bitcast.475), kind=kLoop, calls=%fused_computation.355 | loop fusion | bytes 15138816 | tf_op jit(solution)/shard_map/slice | solution.py:106
  102.8 8.6 %reshape.959 = bf16[4,7,2,22,12,128]{5,4,0,1,3,2:T(8,128)(2,1)} reshape(bf16[1,4,7,44,1536]{4,1,2,0,3:T(4,128)(2,1)} %get-tuple-element.29) | data formatting | bytes 7569408 | tf_op jit(solution)/shard_map/squeeze | solution.py:106
  111.5 10.1 %copy.222 = bf16[4,7,2,22,12,128]{5,2,4,3,1,0:T(2,128)(2,1)} copy(bf16[4,7,2,22,12,128]{5,4,0,1,3,2:T(8,128)(2,1)} %reshape.959) | data formatting | bytes 7569408 | tf_op jit(solution)/shard_map/squeeze | solution.py:106
  121.6 13.1 %gather_fusion.3 = bf16[4,7,2,22,12,128]{5,2,4,3,1,0:T(2,128)(2,1)} fusion(bf16[4,7,2,22,12,128]{5,2,4,3,1,0:T(2,128)(2,1)} %copy.222, s32[1024]{0:T(1024)S(1)} %get-tuple-element.182), kind=kCustom, calls=%fused_computation.3 | custom fusion | bytes 7569424 | tf_op jit(solution)/shard_map/gather | solution.py:115
  134.6 12.7 %gather_fusion.2 = bf16[4,7,2,22,12,128]{5,2,4,3,1,0:T(2,128)(2,1)} fusion(bf16[4,7,2,22,12,128]{5,2,4,3,1,0:T(2,128)(2,1)} %copy.222, s32[1024]{0:T(1024)S(1)} %pad_clamp_fusion.2), kind=kCustom, calls=%fused_computation.2 | custom fusion | bytes 7569424 | tf_op jit(solution)/shard_map/gather | solution.py:115
  147.3 8.8 %reshape.958 = bf16[4,7,2,22,12,128]{5,4,0,1,3,2:T(8,128)(2,1)} reshape(bf16[1,4,7,44,1536]{4,1,2,0,3:T(4,128)(2,1)} %get-tuple-element.30) | data formatting | bytes 7569408 | tf_op jit(solution)/shard_map/squeeze | solution.py:107
  156.1 10.2 %copy.219 = bf16[4,7,2,22,12,128]{5,2,4,3,1,0:T(2,128)(2,1)} copy(bf16[4,7,2,22,12,128]{5,4,0,1,3,2:T(8,128)(2,1)} %reshape.958) | data formatting | bytes 7569408 | tf_op jit(solution)/shard_map/squeeze | solution.py:107
  166.2 12.5 %gather_fusion.1 = bf16[4,7,2,22,12,128]{5,2,4,3,1,0:T(2,128)(2,1)} fusion(bf16[4,7,2,22,12,128]{5,2,4,3,1,0:T(2,128)(2,1)} %copy.219, s32[1024]{0:T(1024)S(1)} %pad_clamp_fusion.2), kind=kCustom, calls=%fused_computation.1 | custom fusion | bytes 7569424 | tf_op jit(solution)/shard_map/gather | solution.py:116
  178.8 12.7 %gather_fusion.5 = bf16[4,7,2,22,12,128]{5,2,4,3,1,0:T(2,128)(2,1)} fusion(bf16[4,7,2,22,12,128]{5,2,4,3,1,0:T(2,128)(2,1)} %copy.219, s32[1024]{0:T(1024)S(1)} %get-tuple-element.182), kind=kCustom, calls=%fused_computation.5 | custom fusion | bytes 7569424 | tf_op jit(solution)/shard_map/gather | solution.py:116
  191.5 12.6 %gather_fusion.4 = bf16[4,7,2,22,12,128]{5,2,4,3,1,0:T(2,128)(2,1)} fusion(bf16[4,7,2,22,12,128]{5,2,4,3,1,0:T(2,128)(2,1)} %copy.222, s32[1024]{0:T(1024)S(1)} %get-tuple-element.181), kind=kCustom, calls=%fused_computation.4 | custom fusion | bytes 7569424 | tf_op jit(solution)/shard_map/gather | solution.py:115
  204.1 12.6 %gather_fusion.6 = bf16[4,7,2,22,12,128]{5,2,4,3,1,0:T(2,128)(2,1)} fusion(bf16[4,7,2,22,12,128]{5,2,4,3,1,0:T(2,128)(2,1)} %copy.219, s32[1024]{0:T(1024)S(1)} %get-tuple-element.181), kind=kCustom, calls=%fused_computation.6 | custom fusion | bytes 7569424 | tf_op jit(solution)/shard_map/gather | solution.py:116
  216.7 4.7 %fusion.154 = (bf16[4,1,2,22,12,128]{5,2,4,3,1,0:T(2,128)(2,1)S(1)}, bf16[4,1,2,22,12,128]{5,2,4,3,1,0:T(2,128)(2,1)S(1)}, bf16[4,1,2,22,12,128]{5,2,4,3,1,0:T(2...) fusion(bf16[4,7,2,22,12,128]{5,2,4,3,1,0:T(2,128)(2,1)} %gather, ...), kind=kLoop, calls=%fused_computation.361 | loop fusion | bytes 7569408 | tf_op jit(solution)/shard_map/slice | solution.py:118
  221.4 2.9 fusion.153
  231.5 3.1 fusion.152
  238.3 2.7 fusion.151
  241.0 2.7 fusion.150
  243.8 3.1 fusion.149
  247.0 1.1 fusion.75
  248.2 4.6 %fusion.76 = (f32[4,2,16,12]{2,3,1,0:T(8,128)S(1)}, f32[4,2,16,12]{2,3,1,0:T(8,128)S(1)}, f32[4,2,16,12]{2,3,1,0:T(8,128)S(1)}, f32[4,2,16,12]{2,3,1,0:T(8,128)S...) fusion(f32[4,1,2,16,12,22]{5,3,4,2,0,1:T(8,128)S(1)} %get-tuple, ...), kind=kLoop, calls=%fused_computation.185 | loop fusion | flops 1188864 | bytes 2549760 | tf_op jit(solution)/shard_map/reduce_sum | solution.py:135
  257.9 1.0 convolution_add_fusion.14
  258.9 1.0 convolution_add_fusion.13
  259.9 1.0 convolution_add_fusion.12
  260.9 1.0 convolution_add_fusion.11
  262.0 1.2 convolution_add_fusion.10
  263.2 1.0 convolution_add_fusion.9
  264.2 1.0 convolution_add_fusion.8
  265.2 1.0 convolution_add_fusion.7
  266.2 1.0 convolution_add_fusion.6
  267.3 1.0 convolution_add_fusion.5
  268.3 1.0 convolution_add_fusion.4
  269.3 1.0 convolution_add_fusion.3
  270.3 1.0 convolution_add_fusion.2
  275.9 4.5 %collective-permute-start.6 = (bf16[4,1,64,16]{3,2,1,0:T(8,128)(2,1)S(1)}, bf16[4,1,64,16]{3,2,1,0:T(8,128)(2,1)S(1)}, u32[]{:S(2)}, u32[]{:S(2)}) collective-permute-start(bf16[4,1,64,16]{3,2,1,0:T(8,128)(2,1)S(1)} %get-tuple-element.128), channel_id=1, source_target_pairs={{0,1},{1,2},{2,3},{3,4},{4,5},{5,6},{6,7},{7,8},{8,9},{9,10},{10,1... | collective-permute-start | bytes 24584 | tf_op jit(solution)/shard_map/ppermute | solution.py:27
  280.4 1.9 collective-permute-start.7
  283.1 2.9 collective-permute-done.7
  286.7 1.0 fusion.155
  288.5 1.3 concatenate.41
  289.8 1.2 fusion.181
  291.0 1.3 concatenate.42
  292.3 1.2 convolution_add_fusion.16
  295.9 1.9 collective-permute-start.8
  297.9 2.4 collective-permute-start.9
  300.3 4.2 %fusion.147 = (bf16[1,3,3,384,384]{4,3,2,1,0:T(8,128)(2,1)S(1)}, bf16[1,3,3,384,384]{4,3,2,1,0:T(8,128)(2,1)S(1)}, bf16[1,3,3,384,384]{4,3,2,1,0:T(8,128)(2,1)S(1)}) fusion(bf16[3,3,3,384,384]{4,3,2,1,0:T(8,128)(2,1)} %param.45), kind=kLoop, calls=%fused_computation.354 | loop fusion | bytes 15925248 | tf_op jit(solution)/shard_map/slice | solution.py:51
  308.2 2.0 fusion.182
  310.2 2.0 convolution_add_fusion.18
  312.3 2.0 convolution_add_fusion.17
  (130 shorter events, 30.0 us)
Async XLA Ops:
  0.0 275.3 %copy-start = (bf16[1536,64]{0,1:T(8,128)(2,1)S(1)}, bf16[1536,64]{0,1:T(8,128)(2,1)}, u32[]{:S(2)}) copy-start(bf16[1536,64]{0,1:T(8,128)(2,1)} %param.38) | copy-start | bytes 589828
  0.0 19.0 %copy-start.22 = (s32[44]{0:T(128)S(1)}, s32[44]{0:T(128)}, u32[]{:S(2)}) copy-start(s32[44]{0:T(128)} %constant.99) | copy-start | bytes 532
  0.0 19.0 %copy-start.20 = (s32[4]{0:T(128)S(1)}, s32[4]{0:T(128)}, u32[]{:S(2)}) copy-start(s32[4]{0:T(128)} %constant.102) | copy-start | bytes 52
  0.0 19.0 %copy-start.21 = (s32[4]{0:T(128)S(1)}, s32[4]{0:T(128)}, u32[]{:S(2)}) copy-start(s32[4]{0:T(128)} %constant.103) | copy-start | bytes 52
  0.0 19.1 %copy-start.19 = (s32[4]{0:T(128)S(1)}, s32[4]{0:T(128)}, u32[]{:S(2)}) copy-start(s32[4]{0:T(128)} %constant.100) | copy-start | bytes 52
  0.0 19.1 %copy-start.14 = (pred[2,16,22]{2,1,0:T(8,128)(4,1)S(1)}, pred[2,16,22]{2,1,0:T(8,128)(4,1)}, u32[]{:S(2)}) copy-start(pred[2,16,22]{2,1,0:T(8,128)(4,1)} %constant.81.clone) | copy-start | bytes 2116
  0.1 19.0 %copy-start.13 = (f32[1536]{0:T(1024)S(1)}, f32[1536]{0:T(1024)}, u32[]{:S(2)}) copy-start(f32[1536]{0:T(1024)} %param.37) | copy-start | bytes 18436
  2.4 16.8 %collective-permute-start = (bf16[2,4,1,32,1536]{4,1,3,2,0:T(4,128)(2,1)S(1)}, bf16[2,4,1,32,1536]{4,1,3,2,0:T(4,128)(2,1)}, u32[]{:S(2)}, u32[]{:S(2)}) collective-permute-start(bf16[2,4,1,32,1536]{4,1,3,2,0:T(4,128)(2,1)S(1)} %pad_maximum_fusion), channel_id=1, source_target_pairs={{0,3},{1,4},{2,5},{3,6},{4,7},{5,8},{6,9},{7,10},{8,11},{9,12},{10... | collective-permute-start | bytes 2359304 | tf_op jit(solution)/shard_map/ppermute | solution.py:16
  7.9 53.4 %collective-permute-start.1 = (bf16[2,4,1,32,1536]{4,1,3,2,0:T(4,128)(2,1)S(1)}, bf16[2,4,1,32,1536]{4,1,3,2,0:T(4,128)(2,1)}, u32[]{:S(2)}, u32[]{:S(2)}) collective-permute-start(bf16[2,4,1,32,1536]{4,1,3,2,0:T(4,128)(2,1)S(1)} %pad_maximum_fusion), channel_id=1, source_target_pairs={{0,2},{1,3},{2,4},{3,5},{4,6},{5,7},{6,8},{7,9},{8,10},{9,11},{10,... | collective-permute-start | bytes 2359304 | tf_op jit(solution)/shard_map/ppermute | solution.py:16
  11.0 63.8 %collective-permute-start.2 = (bf16[2,4,1,32,1536]{4,1,3,2,0:T(4,128)(2,1)S(1)}, bf16[2,4,1,32,1536]{4,1,3,2,0:T(4,128)(2,1)}, u32[]{:S(2)}, u32[]{:S(2)}) collective-permute-start(bf16[2,4,1,32,1536]{4,1,3,2,0:T(4,128)(2,1)S(1)} %pad_maximum_fusion), channel_id=1, source_target_pairs={{0,1},{1,2},{2,3},{3,4},{4,5},{5,6},{6,7},{7,8},{8,9},{9,10},{10,1... | collective-permute-start | bytes 2359304 | tf_op jit(solution)/shard_map/ppermute | solution.py:16
  13.3 65.1 %collective-permute-start.3 = (bf16[2,4,1,32,1536]{4,1,3,2,0:T(4,128)(2,1)S(1)}, bf16[2,4,1,32,1536]{4,1,3,2,0:T(4,128)(2,1)}, u32[]{:S(2)}, u32[]{:S(2)}) collective-permute-start(bf16[2,4,1,32,1536]{4,1,3,2,0:T(4,128)(2,1)S(1)} %pad_maximum_fusion), channel_id=1, source_target_pairs={{1,0},{2,1},{3,2},{4,3},{5,4},{6,5},{7,6},{8,7},{9,8},{10,9},{11,1... | collective-permute-start | bytes 2359304 | tf_op jit(solution)/shard_map/ppermute | solution.py:16
  16.3 64.5 %collective-permute-start.4 = (bf16[2,4,1,32,1536]{4,1,3,2,0:T(4,128)(2,1)S(1)}, bf16[2,4,1,32,1536]{4,1,3,2,0:T(4,128)(2,1)S(1)}, u32[]{:S(2)}, u32[]{:S(2)}) collective-permute-start(bf16[2,4,1,32,1536]{4,1,3,2,0:T(4,128)(2,1)S(1)} %pad_maximum_fusion), channel_id=1, source_target_pairs={{2,0},{3,1},{4,2},{5,3},{6,4},{7,5},{8,6},{9,7},{10,8},{11,9},{12,... | collective-permute-start | bytes 2359304 | tf_op jit(solution)/shard_map/ppermute | solution.py:16
  19.2 62.7 %collective-permute-start.5 = (bf16[2,4,1,32,1536]{4,1,3,2,0:T(4,128)(2,1)S(1)}, bf16[2,4,1,32,1536]{4,1,3,2,0:T(4,128)(2,1)S(1)}, u32[]{:S(2)}, u32[]{:S(2)}) collective-permute-start(bf16[2,4,1,32,1536]{4,1,3,2,0:T(4,128)(2,1)S(1)} %pad_maximum_fusion), channel_id=1, source_target_pairs={{3,0},{4,1},{5,2},{6,3},{7,4},{8,5},{9,6},{10,7},{11,8},{12,9},{13... | collective-permute-start | bytes 2359304 | tf_op jit(solution)/shard_map/ppermute | solution.py:16
  216.7 4.7 %copy-start.5 = (bf16[4,7,2,22,12,128]{5,2,4,3,1,0:T(2,128)(2,1)S(1)}, bf16[4,7,2,22,12,128]{5,2,4,3,1,0:T(2,128)(2,1)}, u32[]{:S(2)}) copy-start(bf16[4,7,2,22,12,128]{5,2,4,3,1,0:T(2,128)(2,1)} %gather_fusion.3) | copy-start | bytes 11354116
  229.4 2.1 copy-start.4
  236.2 2.1 copy-start.3
  238.3 2.8 copy-start.2
  241.0 2.8 copy-start.1
  273.4 1.1 copy-start.6
  273.4 1.1 copy-start.10
  273.4 1.6 copy-start.11
  274.0 1.3 copy-start.23
  274.0 1.8 copy-start.17
  274.0 1.8 copy-start.18
  274.0 8.3 %copy-start.8 = (bf16[3,3,3,16,384]{4,3,2,1,0:T(8,128)(2,1)S(1)}, bf16[3,3,3,16,384]{4,3,2,1,0:T(8,128)(2,1)}, u32[]{:S(2)}) copy-start(bf16[3,3,3,16,384]{4,3,2,1,0:T(8,128)(2,1)} %param.42) | copy-start | bytes 995332
  275.9 7.2 %collective-permute-start.6 = (bf16[4,1,64,16]{3,2,1,0:T(8,128)(2,1)S(1)}, bf16[4,1,64,16]{3,2,1,0:T(8,128)(2,1)S(1)}, u32[]{:S(2)}, u32[]{:S(2)}) collective-permute-start(bf16[4,1,64,16]{3,2,1,0:T(8,128)(2,1)S(1)} %get-tuple-element.128), channel_id=1, source_target_pairs={{0,1},{1,2},{2,3},{3,4},{4,5},{5,6},{6,7},{7,8},{8,9},{9,10},{10,1... | collective-permute-start | bytes 24584 | tf_op jit(solution)/shard_map/ppermute | solution.py:27
  280.4 5.6 %collective-permute-start.7 = (bf16[4,1,64,16]{3,2,1,0:T(8,128)(2,1)S(1)}, bf16[4,1,64,16]{3,2,1,0:T(8,128)(2,1)S(1)}, u32[]{:S(2)}, u32[]{:S(2)}) collective-permute-start(bf16[4,1,64,16]{3,2,1,0:T(8,128)(2,1)S(1)} %get-tuple-element.129), channel_id=1, source_target_pairs={{1,0},{2,1},{3,2},{4,3},{5,4},{6,5},{7,6},{8,7},{9,8},{10,9},{11,1... | collective-permute-start | bytes 24584 | tf_op jit(solution)/shard_map/ppermute | solution.py:29
  286.0 0.6 copy-start.9
  291.0 4.3 %copy-start.15 = (f32[384]{0:T(512)S(1)}, f32[384]{0:T(512)}, u32[]{:S(2)}) copy-start(f32[384]{0:T(512)} %param.43) | copy-start | bytes 4612
  292.3 2.7 copy-start.7
  292.3 3.3 %copy-start.12 = (f32[384]{0:T(512)S(1)}, f32[384]{0:T(512)}, u32[]{:S(2)}) copy-start(f32[384]{0:T(512)} %param.44) | copy-start | bytes 4612
  295.9 8.6 %collective-permute-start.8 = (bf16[4,1,64,384]{3,2,1,0:T(8,128)(2,1)S(1)}, bf16[4,1,64,384]{3,2,1,0:T(8,128)(2,1)S(1)}, u32[]{:S(2)}, u32[]{:S(2)}) collective-permute-start(bf16[4,1,64,384]{3,2,1,0:T(8,128)(2,1)S(1)} %get-tuple-element.121), channel_id=1, source_target_pairs={{0,1},{1,2},{2,3},{3,4},{4,5},{5,6},{6,7},{7,8},{8,9},{9,10},{10,1... | collective-permute-start | bytes 589832 | tf_op jit(solution)/shard_map/ppermute | solution.py:27
  297.9 7.0 %collective-permute-start.9 = (bf16[4,1,64,384]{3,2,1,0:T(8,128)(2,1)S(1)}, bf16[4,1,64,384]{3,2,1,0:T(8,128)(2,1)S(1)}, u32[]{:S(2)}, u32[]{:S(2)}) collective-permute-start(bf16[4,1,64,384]{3,2,1,0:T(8,128)(2,1)S(1)} %get-tuple-element.122), channel_id=1, source_target_pairs={{1,0},{2,1},{3,2},{4,3},{5,4},{6,5},{7,6},{8,7},{9,8},{10,9},{11,1... | collective-permute-start | bytes 589832 | tf_op jit(solution)/shard_map/ppermute | solution.py:29
  312.2 2.0 copy-start.16
where the time goes:
time: 321 us; the launch traced here: 315 us
  local copies, waits for them, and re-layouts  181 us (56%)
  waiting for transfers between devices  53 us (17%)
  matrix products  40.5 us (13%)
  starting transfers between devices  27.2 us (8%)
  other arithmetic  11.8 us (4%)
    ppermute x6, waiting for transfers between devices, shifted(): return lax.ppermute(block, axis, route)  49.8 us
    gather x3, local copies, waits for them, and re-layouts, shards(): key_frames = keys_ext[frame_start + a]  38.4 us
    gather x3, local copies, waits for them, and re-layouts, shards(): value_frames = values_ext[frame_start + a]  37.8 us
    dot_general x21, matrix products, shards(): jnp.einsum('finwhv,finvhd->finwhd', block_probs, value_blocks[index], pre...  20.9 us
    squeeze x2, local copies, waits for them, and re-layouts, shards(): values_ext = tiled_pair[1]  18.9 us
    squeeze x2, local copies, waits for them, and re-layouts, shards(): keys_ext = tiled_pair[0]  18.7 us
    ppermute x6, starting transfers between devices, shifted(): return lax.ppermute(block, axis, route)  16.4 us
    unnamed x61, local copies, waits for them, and re-layouts  13.2 us
  transfers between devices with their start and end apart: 10, of which 4 were waited for; matrix products, arithmetic and copies ran while one was open for 6% of the time, Pallas kernels for 0%

commit v1 on v0

v1 whole, which is shorter than its diff:
```python
import functools

import jax
import jax.numpy as jnp
from jax import lax
from jax.experimental import pallas as pl
from jax.experimental.pallas import tpu as pltpu
from jax.sharding import PartitionSpec as P

HEADS = 12
LAT = 16
GROUP = 4
HPD = HEADS // GROUP
HD = 128
FR = 4
COLS = 32
TOK = FR * COLS
ROWS_EXT = GROUP + 6
KEYS = FR * 7 * COLS
C = 384
NEG = -1e30


def attend_kernel(
    n_rows,
    stream_ref,
    q_ref,
    k_ref,
    v_ref,
    mods_ref,
    hw_ref,
    small_ref,
    out_ref,
    qb,
    kb,
    vb,
    ob,
    attn,
    bias,
    gbuf,
    own_sem,
    s1,
    r1,
    s2,
    r2,
    s3,
    r3,
    s4,
    r4,
):
    row = lax.axis_index("row")
    g = row // GROUP
    j = row % GROUP
    groups = n_rows // GROUP
    has_up = g > 0
    has_down = g < groups - 1
    first = row == 0
    last = row == n_rows - 1

    def head_cols(p, h):
        return pl.ds(pl.multiple_of((p * HPD + h) * HD, HD), HD)

    srcs = (k_ref, v_ref, q_ref)

    def level_dst(x, h, idx):
        if x == 2:
            return qb.at[h, idx]
        return (kb, vb)[x].at[h, :, idx + 3]

    own = []
    for h in range(HPD):
        for x in range(3):
            cp = pltpu.make_async_copy(
                srcs[x].at[:, :, head_cols(j, h)], level_dst(x, h, j), own_sem.at[x, h]
            )
            cp.start()
            own.append(cp)

    barrier = pltpu.get_barrier_semaphore()
    for d in range(1, GROUP):
        pl.semaphore_signal(barrier, inc=1, device_id={"row": g * GROUP + (j + d) % GROUP})

    @pl.when(has_up)
    def _():
        pl.semaphore_signal(barrier, inc=1, device_id={"row": row - GROUP})

    @pl.when(has_down)
    def _():
        pl.semaphore_signal(barrier, inc=1, device_id={"row": row + GROUP})

    cross_up = jnp.logical_and(j == 0, has_up)
    cross_down = jnp.logical_and(j == GROUP - 1, has_down)

    @pl.when(cross_up)
    def _():
        pl.semaphore_signal(barrier, inc=1, device_id={"row": row - 1})

    @pl.when(cross_down)
    def _():
        pl.semaphore_signal(barrier, inc=1, device_id={"row": row + 1})

    one = jnp.int32(1)
    zero = jnp.int32(0)
    expected = (
        3
        + jnp.where(has_up, one, zero)
        + jnp.where(has_down, one, zero)
        + jnp.where(cross_up, one, zero)
        + jnp.where(cross_down, one, zero)
    )
    pl.semaphore_wait(barrier, expected)

    def level_copy(x, h, d):
        p = (j + d) % GROUP
        return pltpu.make_async_remote_copy(
            src_ref=srcs[x].at[:, :, head_cols(p, h)],
            dst_ref=level_dst(x, h, j),
            send_sem=s1.at[x, h, d - 1],
            recv_sem=r1.at[x, h, d - 1],
            device_id={"row": g * GROUP + p},
        )

    for h in range(HPD):
        for x in range(2):
            for d in (2, 1, 3):
                level_copy(x, h, d).start()
    for h in range(HPD):
        for d in (2, 1, 3):
            level_copy(2, h, d).start()

    def edge_copy(x, h, up):
        buf = (kb, vb)[x]
        if up:
            src, dst, dev = buf.at[h, :, pl.ds(3, 3)], buf.at[h, :, pl.ds(7, 3)], row - GROUP
        else:
            src, dst, dev = buf.at[h, :, pl.ds(4, 3)], buf.at[h, :, pl.ds(0, 3)], row + GROUP
        way = 0 if up else 1
        return pltpu.make_async_remote_copy(
            src_ref=src,
            dst_ref=dst,
            send_sem=s2.at[x, h, way],
            recv_sem=r2.at[x, h, way],
            device_id={"row": dev},
        )

    tok_i = lax.broadcasted_iota(jnp.int32, (TOK, KEYS), 0)
    key_i = lax.broadcasted_iota(jnp.int32, (TOK, KEYS), 1)
    t = tok_i >> 5
    w = tok_i & 31
    span = 7 * COLS
    f = (
        jnp.where(key_i >= span, 1, 0)
        + jnp.where(key_i >= 2 * span, 1, 0)
        + jnp.where(key_i >= 3 * span, 1, 0)
    )
    fs = jnp.clip(t - 1, 0, FR - 3)
    cs = jnp.clip(w - 3, 0, COLS - 7)
    vcol = key_i & 31
    ok = (f >= fs) & (f < fs + 3) & (vcol >= cs) & (vcol < cs + 7)
    bias[...] = jnp.where(ok, 0.0, NEG)

    empty = jnp.zeros((HPD, FR, 3, COLS, HD), jnp.bfloat16)

    @pl.when(jnp.logical_not(has_up))
    def _():
        kb[:, :, 0:3] = empty
        vb[:, :, 0:3] = empty

    @pl.when(jnp.logical_not(has_down))
    def _():
        kb[:, :, 7:10] = empty
        vb[:, :, 7:10] = empty

    @pl.when(first)
    def _():
        gbuf[0] = jnp.zeros((TOK, 128), jnp.bfloat16)

    @pl.when(last)
    def _():
        gbuf[2] = jnp.zeros((TOK, 128), jnp.bfloat16)

    for cp in own:
        cp.wait()

    for h in range(HPD):
        for x in range(2):
            for d in range(1, GROUP):
                level_copy(x, h, d).wait_recv()

            @pl.when(has_up)
            def _():
                edge_copy(x, h, True).start()

            @pl.when(has_down)
            def _():
                edge_copy(x, h, False).start()

    key_row = lax.broadcasted_iota(jnp.int32, (1, KEYS), 1)
    fr = (
        jnp.where(key_row >= span, 1, 0)
        + jnp.where(key_row >= 2 * span, 1, 0)
        + jnp.where(key_row >= 3 * span, 1, 0)
    )
    rel_row = (key_row >> 5) - 7 * fr + (GROUP * g - 3)

    def out_copy(h, d):
        p = (j + d) % GROUP
        return pltpu.make_async_remote_copy(
            src_ref=ob.at[h, p],
            dst_ref=attn.at[j * HPD + h],
            send_sem=s3.at[h, d - 1],
            recv_sem=r3.at[h, d - 1],
            device_id={"row": g * GROUP + p},
        )

    for h in range(HPD):
        for d in range(1, GROUP):
            level_copy(2, h, d).wait_recv()
        for x in range(2):

            @pl.when(has_down)
            def _():
                edge_copy(x, h, True).wait_recv()

            @pl.when(has_up)
            def _():
                edge_copy(x, h, False).wait_recv()

        def one_row(i, carry):
            qm = qb[h, i].reshape(TOK, HD)
            km = kb[h, :, pl.ds(i, 7)].reshape(KEYS, HD)
            vm = vb[h, :, pl.ds(i, 7)].reshape(KEYS, HD)
            s = lax.dot_general(
                qm, km, (((1,), (1,)), ((), ())), preferred_element_type=jnp.float32
            )
            src_row = rel_row + i
            row_bias = jnp.where((src_row >= 0) & (src_row < n_rows), 0.0, NEG)
            s = s * (HD**-0.5) + (bias[...] + row_bias)
            m = jnp.max(s, axis=1, keepdims=True)
            e = jnp.exp(s - m)
            l = jnp.sum(e, axis=1, keepdims=True)
            pr = (e * (1.0 / l)).astype(jnp.bfloat16)
            o = jnp.dot(pr, vm, preferred_element_type=jnp.float32)
            ob[h, i] = o.astype(jnp.bfloat16)
            return carry

        lax.fori_loop(0, GROUP, one_row, 0)
        for d in (2, 1, 3):
            out_copy(h, d).start()
        attn[j * HPD + h] = ob[h, j]

    for h in range(HPD):
        for d in range(1, GROUP):
            out_copy(h, d).wait_recv()

    attn_all = jnp.concatenate([attn[c] for c in range(HEADS)], axis=-1)
    resid = stream_ref[...].astype(jnp.float32) + mods_ref[0:1, :] * attn_all.astype(jnp.float32)
    center = resid - jnp.mean(resid, axis=-1, keepdims=True)
    spread = jnp.mean(center * center, axis=-1, keepdims=True)
    normed = center * lax.rsqrt(spread + 1e-06) * (1.0 + mods_ref[2:3, :]) + mods_ref[1:2, :]
    patch = jnp.dot(
        normed.astype(jnp.bfloat16), hw_ref[...], preferred_element_type=jnp.float32
    )
    patch = patch + small_ref[0:1, :]
    latent = (patch * small_ref[1:2, :] + small_ref[2:3, :]).astype(jnp.bfloat16)

    dst_l = lax.broadcasted_iota(jnp.int32, (4 * LAT, 128), 1)
    src_l = lax.broadcasted_iota(jnp.int32, (4 * LAT, 128), 0)
    part = (dst_l >> 4) & 3
    want = ((dst_l >> 6) * 2 + (1 - (part & 1))) * LAT + (dst_l & 15)
    pick = jnp.where(src_l == want, 1.0, 0.0).astype(jnp.bfloat16)
    spreadout = jnp.dot(latent, pick, preferred_element_type=jnp.float32)
    lane = lax.broadcasted_iota(jnp.int32, (TOK, 128), 1)
    col = lax.broadcasted_iota(jnp.int32, (TOK, 128), 0) & 31
    lane_part = (lane >> 4) & 3
    before = jnp.where(col == 0, 0.0, pltpu.roll(spreadout, 1, 0))
    after = jnp.where(col == COLS - 1, 0.0, pltpu.roll(spreadout, TOK - 1, 0))
    cells = jnp.where(lane_part == 0, before, jnp.where(lane_part == 3, after, spreadout))
    gbuf[1] = cells.astype(jnp.bfloat16)

    def latent_copy(up):
        way = 0 if up else 1
        return pltpu.make_async_remote_copy(
            src_ref=gbuf.at[1],
            dst_ref=gbuf.at[2 if up else 0],
            send_sem=s4.at[way],
            recv_sem=r4.at[way],
            device_id={"row": row - 1 if up else row + 1},
        )

    @pl.when(jnp.logical_not(first))
    def _():
        latent_copy(True).start()

    @pl.when(jnp.logical_not(last))
    def _():
        latent_copy(False).start()

    for h in range(HPD):
        for x in range(3):
            for d in range(1, GROUP):
                level_copy(x, h, d).wait_send()
        for x in range(2):

            @pl.when(has_up)
            def _():
                edge_copy(x, h, True).wait_send()

            @pl.when(has_down)
            def _():
                edge_copy(x, h, False).wait_send()

        for d in range(1, GROUP):
            out_copy(h, d).wait_send()

    @pl.when(jnp.logical_not(first))
    def _():
        latent_copy(True).wait_send()
        latent_copy(False).wait_recv()

    @pl.when(jnp.logical_not(last))
    def _():
        latent_copy(False).wait_send()
        latent_copy(True).wait_recv()

    out_ref[...] = gbuf[...]


def decode_kernel(n_rows, cells_ref, cw_ref, vec_ref, w_ref, out_ref, w4, var, acc, wide):
    step = pl.program_id(0)
    a = step // 3
    b = step % 3

    @pl.when(step == 0)
    def _():
        row = lax.axis_index("row")
        w4[...] = jnp.zeros(w4.shape, jnp.bfloat16)
        for ab in range(9):
            w4[ab * 64 : ab * 64 + 48, 0:C] = cw_ref[ab]
            w4[ab * 64 + 16 : ab * 64 + 64, C : 2 * C] = cw_ref[ab]
        six = jnp.concatenate([cells_ref[i] for i in range(3)], axis=-1)
        col = lax.broadcasted_iota(jnp.int32, (TOK, C), 0) & 31
        zeros = jnp.zeros((2 * COLS, C), jnp.bfloat16)
        pad = jnp.zeros((2 * COLS, 192), jnp.bfloat16)
        for y in range(4):
            rows3 = six[:, y * 64 : y * 64 + 192]
            padded = jnp.concatenate([pad, rows3], axis=0)
            x = jnp.concatenate(
                [padded[i * COLS : i * COLS + TOK] for i in range(3)], axis=-1
            )
            h = jnp.dot(x, w4[...], preferred_element_type=jnp.float32)
            acts = []
            for q in range(2):
                hidden = (h[:, q * C : (q + 1) * C] + vec_ref[0:1, :]).astype(jnp.bfloat16)
                hidden = hidden.astype(jnp.float32)
                if y in (1, 2):
                    at = ((y - 1) * 2 + q) * TOK
                    acc[at : at + TOK, :] = hidden + vec_ref[2:3, :]
                ms = jnp.mean(hidden * hidden, axis=-1, keepdims=True)
                scaled = hidden * lax.rsqrt(ms + 1e-06) * vec_ref[1:2, :]
                act = scaled / (1.0 + jnp.exp(-scaled))
                if y == 0:
                    act = jnp.where(row > 0, act, 0.0)
                if y == 3:
                    act = jnp.where(row < n_rows - 1, act, 0.0)
                acts.append(act)
            before = jnp.where(col == 0, 0.0, pltpu.roll(acts[1], 1, 0))
            after = jnp.where(col == COLS - 1, 0.0, pltpu.roll(acts[0], TOK - 1, 0))
            for i, piece in enumerate((before, acts[0], acts[1], after)):
                var[i, y, 0 : 2 * COLS] = zeros
                var[i, y, 2 * COLS :] = piece.astype(jnp.bfloat16)

    start = pl.multiple_of(a * COLS, COLS)
    phases = []
    for y in range(2):
        taps = [var[i, y + b, pl.ds(start, TOK)] for i in range(4)]
        for q in range(2):
            phases.append(jnp.concatenate(taps[q : q + 3], axis=-1))
    lhs = jnp.concatenate(phases, axis=0)
    acc[...] += jnp.dot(lhs, w_ref[0], preferred_element_type=jnp.float32)

    @pl.when(step == 8)
    def _():
        for y in range(2):
            for q in range(2):
                for t in range(FR):
                    at = (y * 2 + q) * TOK + t * COLS
                    for c in range(3):
                        wide[t, y, c, pl.ds(q, COLS, stride=2), :] = acc[
                            at : at + COLS, c * 128 : (c + 1) * 128
                        ]
        for c in range(3):
            out_ref[:, :, :, c * 128 : (c + 1) * 128] = wide[:, :, c].astype(jnp.bfloat16)


def shards(
    n_rows,
    stream,
    query,
    key,
    value,
    attn_gate,
    shift_mod,
    scale_mod,
    head_weight,
    head_bias,
    latent_mean,
    latent_std,
    conv_in_weight,
    conv_in_bias,
    norm_gain,
    conv_weight,
    conv_bias,
):
    width = query.shape[-1]
    flat = (FR, COLS, width)
    mods = jnp.stack([attn_gate, shift_mod, scale_mod])
    small = jnp.stack([head_bias, jnp.tile(latent_std, 4), jnp.tile(latent_mean, 4)])
    vecs = jnp.stack([conv_in_bias, norm_gain, conv_bias])
    vmem = pl.BlockSpec(memory_space=pltpu.VMEM)
    anywhere = pl.BlockSpec(memory_space=pl.ANY)
    dma = pltpu.SemaphoreType.DMA
    bf = jnp.bfloat16
    cells = pl.pallas_call(
        functools.partial(attend_kernel, n_rows),
        out_shape=jax.ShapeDtypeStruct((3, TOK, 128), bf),
        in_specs=[vmem, anywhere, anywhere, anywhere, vmem, vmem, vmem],
        out_specs=vmem,
        scratch_shapes=[
            pltpu.VMEM((HPD, GROUP, FR, COLS, HD), bf),
            pltpu.VMEM((HPD, FR, ROWS_EXT, COLS, HD), bf),
            pltpu.VMEM((HPD, FR, ROWS_EXT, COLS, HD), bf),
            pltpu.VMEM((HPD, GROUP, TOK, HD), bf),
            pltpu.VMEM((HEADS, TOK, HD), bf),
            pltpu.VMEM((TOK, KEYS), jnp.float32),
            pltpu.VMEM((3, TOK, 128), bf),
            dma((3, HPD)),
            dma((3, HPD, 3)),
            dma((3, HPD, 3)),
            dma((2, HPD, 2)),
            dma((2, HPD, 2)),
            dma((HPD, 3)),
            dma((HPD, 3)),
            dma((2,)),
            dma((2,)),
        ],
        compiler_params=pltpu.CompilerParams(
            collective_id=0, has_side_effects=True, vmem_limit_bytes=24 << 20
        ),
        name="attend",
    )(
        stream.reshape(TOK, width),
        query.reshape(flat),
        key.reshape(flat),
        value.reshape(flat),
        mods,
        head_weight,
        small,
    )
    whole = lambda *shape: pl.BlockSpec(shape, lambda s: (0,) * len(shape))
    return pl.pallas_call(
        functools.partial(decode_kernel, n_rows),
        out_shape=jax.ShapeDtypeStruct((FR, 2, 2 * COLS, C), bf),
        grid=(9,),
        in_specs=[
            whole(3, TOK, 128),
            whole(9, 3 * LAT, C),
            whole(3, C),
            pl.BlockSpec((1, 3 * C, C), lambda s: (s, 0, 0)),
        ],
        out_specs=whole(FR, 2, 2 * COLS, C),
        scratch_shapes=[
            pltpu.VMEM((576, 2 * C), bf),
            pltpu.VMEM((4, 4, 2 * COLS + TOK, C), bf),
            pltpu.VMEM((4 * TOK, C), jnp.float32),
            pltpu.VMEM((FR, 2, 3, 2 * COLS, 128), jnp.float32),
        ],
        compiler_params=pltpu.CompilerParams(vmem_limit_bytes=32 << 20),
        name="decode",
    )(
        cells,
        conv_in_weight.reshape(9, 3 * LAT, C),
        vecs,
        conv_weight.reshape(9, 3 * C, C),
    )


def solution(mesh):
    cut = P("video", "row", None, None)
    part = P("video")
    return jax.shard_map(
        functools.partial(shards, mesh.shape["row"]),
        mesh=mesh,
        in_specs=(cut,) * 4 + (part,) * 3 + (P(),) * 9,
        out_specs=cut,
        check_vma=False,
    )
```

time: 321 us -> 57.9 us (0.18); the launches traced: 315 us -> 57.3 us
  local copies, waits for them, and re-layouts: 181 us -> 15 us
  waiting for transfers between devices: 53 us -> 0 us
  Pallas kernels: 0 us -> 41.6 us
  matrix products: 40.5 us -> 0 us
  starting transfers between devices: 27.2 us -> 0 us
  other arithmetic: 11.8 us -> 0.7 us
    gather x7 -> x0, local copies, waits for them, and re-layouts: 88.4 us -> none  [the longest x3 38.4 us: shards(): key_frames = keys_ext[frame_start + a]]
    ppermute x10 -> x0, waiting for transfers between devices: 53 us -> none  [the longest x6 49.8 us: shifted(): return lax.ppermute(block, axis, route)]
    pallas_call x0 -> x2, Pallas kernels: none -> 41.6 us  [the longest x1 31.8 us: shards(): pl.pallas_call(functools.partial(attend_kernel, n_rows), out_shape=jax.Sh...]
    dot_general x49 -> x0, matrix products: 40.5 us -> none  [the longest x21 20.9 us: shards(): jnp.einsum('finwhv,finvhd->finwhd', block_probs, value_blocks[index], pre...]
    squeeze x4 -> x0, local copies, waits for them, and re-layouts: 37.6 us -> none  [the longest x2 18.9 us: shards(): values_ext = tiled_pair[1]]
    slice x13 -> x0, local copies, waits for them, and re-layouts: 33.6 us -> none  [the longest x3 10.7 us: shards(): key_block = key_frames[:, r:r + own_rows]]
    ppermute x10 -> x0, starting transfers between devices: 27.2 us -> none  [the longest x6 16.4 us: shifted(): return lax.ppermute(block, axis, route)]
    reduce_sum x5 -> x0, other arithmetic: 6.37 us -> none  [the longest x2 5.72 us: shards(): jnp.sum(jnp.exp(scores[index] - peak), axis=5, keepdims=True)]
  transfers between devices with their start and end apart: 10 -> 0, of which waited for: 4 -> 0; matrix products, arithmetic and copies ran while one was open for 6% -> 0% of each run, Pallas kernels for 0% -> 0%
where the time goes in v1:
time: 57.9 us; the launch traced here: 57.3 us
  Pallas kernels  41.6 us (72%)
  local copies, waits for them, and re-layouts  15 us (26%)
  other arithmetic  0.7 us (1%)
    pallas_call x1, Pallas kernels, shards(): pl.pallas_call(functools.partial(attend_kernel, n_rows), out_shape=jax.Sh...  31.8 us
    pallas_call x1, Pallas kernels, shards(): pl.pallas_call(functools.partial(decode_kernel, n_rows), out_shape=jax.Sh...  9.71 us
    unnamed x13, local copies, waits for them, and re-layouts  9.36 us
    another operation x3, local copies, waits for them, and re-layouts, shards(): mods = jnp.stack([attn_gate, shift_mod, scale_mod])  2.11 us
    another operation x3, local copies, waits for them, and re-layouts, shards(): vecs = jnp.stack([conv_in_bias, norm_gain, conv_bias])  2.05 us

profile of v1, /device:TPU:1, one launch (start us, length us, event | category | flops | bytes accessed | tf_op | source)
XLA Modules:
  0.0 57.3 jit_solution(16273075371753194902)
XLA Ops:
  0.0 1.1 %copy.17.hw_ref = bf16[1536,64]{1,0:T(8,128)(2,1)S(1)} copy(bf16[1536,64]{0,1:T(8,128)(2,1)} %param.23) | data formatting | bytes 393216 | tf_op args[7]
  1.2 0.7 %stack.30 = f32[1,1536]{1,0:T(1,128)S(1)} reshape(f32[1536]{0:T(1024)} %param.20) | data formatting | bytes 12288 | tf_op jit(solution)/shard_map/stack | solution.py:417
  1.9 0.7 %stack.31 = f32[1,1536]{1,0:T(1,128)S(1)} reshape(f32[1536]{0:T(1024)} %param.21) | data formatting | bytes 12288 | tf_op jit(solution)/shard_map/stack | solution.py:417
  2.6 0.7 %stack.32 = f32[1,1536]{1,0:T(1,128)S(1)} reshape(f32[1536]{0:T(1024)} %param.22) | data formatting | bytes 12288 | tf_op jit(solution)/shard_map/stack | solution.py:417
  3.3 0.7 %tile.4 = f32[4,16]{1,0:T(4,128)S(1)} broadcast(f32[16]{0:T(128)} %param.26), dimensions={1} | broadcast | bytes 320 | tf_op jit(solution)/shard_map/tile | solution.py:418
  3.9 0.1 stack_tile.6
  4.0 0.7 %tile.5 = f32[4,16]{1,0:T(4,128)S(1)} broadcast(f32[16]{0:T(128)} %param.25), dimensions={1} | broadcast | bytes 320 | tf_op jit(solution)/shard_map/tile | solution.py:418
  4.7 0.1 stack_tile.7
  4.8 0.7 %pad_maximum_fusion.2.small_ref = f32[3,64]{1,0:T(4,128)S(1)} fusion(f32[1,64]{1,0:T(1,128)S(1)} %stack_tile.7, f32[1,64]{1,0:T(1,128)S(1)} %stack_tile.6, f32[1,64]{1,0:T(1,128)} %bitcast.13), kind=kLoop, calls=%fused_computation.2 | loop fusion | flops 384 | bytes 1536 | tf_op jit(solution)/shard_map/stack | solution.py:418
  5.4 0.0 copy-start.1
  5.4 1.0 %copy-done.1 = bf16[4,1,32,1536]{3,2,1,0:T(8,128)(2,1)S(1)} copy-done((bf16[4,1,32,1536]{3,2,1,0:T(8,128)(2,1)S(1)}, bf16[4,1,32,1536]{3,2,1,0:T(8,128)(2,1)}, u32[]{:S(2)}) %copy-start.1) | copy-done | bytes 393240
  6.4 0.0 copy-start.2
  6.4 1.0 %copy-done.2 = bf16[4,1,32,1536]{3,2,1,0:T(8,128)(2,1)S(1)} copy-done((bf16[4,1,32,1536]{3,2,1,0:T(8,128)(2,1)S(1)}, bf16[4,1,32,1536]{3,2,1,0:T(8,128)(2,1)}, u32[]{:S(2)}) %copy-start.2) | copy-done | bytes 393240
  7.4 0.0 copy-start.3
  7.4 1.0 %copy-done.3 = bf16[4,1,32,1536]{3,2,1,0:T(8,128)(2,1)S(1)} copy-done((bf16[4,1,32,1536]{3,2,1,0:T(8,128)(2,1)S(1)}, bf16[4,1,32,1536]{3,2,1,0:T(8,128)(2,1)}, u32[]{:S(2)}) %copy-start.3) | copy-done | bytes 393240
  8.4 0.0 copy-start.4
  8.4 1.0 %copy-done.4 = bf16[4,1,32,1536]{3,2,1,0:T(8,128)(2,1)S(1)} copy-done((bf16[4,1,32,1536]{3,2,1,0:T(8,128)(2,1)S(1)}, bf16[4,1,32,1536]{3,2,1,0:T(8,128)(2,1)}, u32[]{:S(2)}) %copy-start.4) | copy-done | bytes 393240
  9.4 31.8 %attend.1.cells_ref = bf16[3,128,128]{2,1,0:T(8,128)(2,1)S(1)} custom-call(bf16[128,1536]{1,0:T(8,128)(2,1)S(1)} %bitcast.8, bf16[4,32,1536]{2,1,0:T(8,128)(2,1)S(1)} %bitcast.9, bf16[4,32,1536]{2,1,0:T(8,128)(2,1)S(1)} %bitcast.10, bf16[4,32,1536]{2,1,0:T(8,128)(2,1)S(1)} %bitcast.11, f32[3,1536]{1,0:T(4,128)S(1)} %pad_maximum_fusion.mods_ref, ...), custom_call_target="tpu_custom_call" | custom-call | tf_op jit(solution)/shard_map/attend/pallas_call | solution.py:424
  41.3 0.7 %stack.36 = f32[1,384]{1,0:T(1,128)S(1)} reshape(f32[384]{0:T(512)} %param.28) | data formatting | bytes 3072 | tf_op jit(solution)/shard_map/stack | solution.py:419
  42.0 0.7 %stack.37 = f32[1,384]{1,0:T(1,128)S(1)} reshape(f32[384]{0:T(512)} %param.29) | data formatting | bytes 3072 | tf_op jit(solution)/shard_map/stack | solution.py:419
  42.6 0.7 %stack.38 = f32[1,384]{1,0:T(1,128)S(1)} reshape(f32[384]{0:T(512)} %param.31) | data formatting | bytes 3072 | tf_op jit(solution)/shard_map/stack | solution.py:419
  43.3 0.0 copy-start
  43.4 3.3 %copy-done = bf16[3,3,3,384,384]{4,3,2,1,0:T(8,128)(2,1)S(1)} copy-done((bf16[3,3,3,384,384]{4,3,2,1,0:T(8,128)(2,1)S(1)}, bf16[3,3,3,384,384]{4,3,2,1,0:T(8,128)(2,1)}, u32[]{:S(2)}) %copy-start) | copy-done | bytes 7962648
  46.6 0.0 copy-start.5
  46.6 1.0 %copy-done.5 = bf16[3,3,3,16,384]{4,3,2,1,0:T(8,128)(2,1)S(1)} copy-done((bf16[3,3,3,16,384]{4,3,2,1,0:T(8,128)(2,1)S(1)}, bf16[3,3,3,16,384]{4,3,2,1,0:T(8,128)(2,1)}, u32[]{:S(2)}) %copy-start.5) | copy-done | bytes 331800
  47.6 9.7 %decode.1 = bf16[4,2,64,384]{3,2,1,0:T(8,128)(2,1)} custom-call(bf16[3,128,128]{2,1,0:T(8,128)(2,1)S(1)} %attend.1.cells_ref, bf16[9,48,384]{2,1,0:T(8,128)(2,1)S(1)} %bitcast.12, f32[3,384]{1,0:T(4,128)S(1)} %pad_maximum_fusion.1.vec_ref, bf16[9,1152,384]{2,1,0:T(8,128)(2,1)S(1)} %bitcast.7), custom_call_target="tpu_custom_call" | custom-call | tf_op jit(solution)/shard_map/decode/pallas_call | solution.py:461
  (2 shorter events, 0.0 us)
Async XLA Ops:
  5.4 1.0 %copy-start.1 = (bf16[4,1,32,1536]{3,2,1,0:T(8,128)(2,1)S(1)}, bf16[4,1,32,1536]{3,2,1,0:T(8,128)(2,1)}, u32[]{:S(2)}) copy-start(bf16[4,1,32,1536]{3,2,1,0:T(8,128)(2,1)} %param.16) | copy-start | bytes 1179652
  6.4 1.0 %copy-start.2 = (bf16[4,1,32,1536]{3,2,1,0:T(8,128)(2,1)S(1)}, bf16[4,1,32,1536]{3,2,1,0:T(8,128)(2,1)}, u32[]{:S(2)}) copy-start(bf16[4,1,32,1536]{3,2,1,0:T(8,128)(2,1)} %param.17) | copy-start | bytes 1179652
  7.4 1.0 %copy-start.3 = (bf16[4,1,32,1536]{3,2,1,0:T(8,128)(2,1)S(1)}, bf16[4,1,32,1536]{3,2,1,0:T(8,128)(2,1)}, u32[]{:S(2)}) copy-start(bf16[4,1,32,1536]{3,2,1,0:T(8,128)(2,1)} %param.18) | copy-start | bytes 1179652
  8.4 1.0 %copy-start.4 = (bf16[4,1,32,1536]{3,2,1,0:T(8,128)(2,1)S(1)}, bf16[4,1,32,1536]{3,2,1,0:T(8,128)(2,1)}, u32[]{:S(2)}) copy-start(bf16[4,1,32,1536]{3,2,1,0:T(8,128)(2,1)} %param.19) | copy-start | bytes 1179652
  43.3 3.3 %copy-start = (bf16[3,3,3,384,384]{4,3,2,1,0:T(8,128)(2,1)S(1)}, bf16[3,3,3,384,384]{4,3,2,1,0:T(8,128)(2,1)}, u32[]{:S(2)}) copy-start(bf16[3,3,3,384,384]{4,3,2,1,0:T(8,128)(2,1)} %param.30) | copy-start | bytes 23887876
  46.6 1.0 %copy-start.5 = (bf16[3,3,3,16,384]{4,3,2,1,0:T(8,128)(2,1)S(1)}, bf16[3,3,3,16,384]{4,3,2,1,0:T(8,128)(2,1)}, u32[]{:S(2)}) copy-start(bf16[3,3,3,16,384]{4,3,2,1,0:T(8,128)(2,1)} %param.27) | copy-start | bytes 995332

commit v2 on v1

--- a/solution.py
+++ b/solution.py
@@ -19,18 +19,47 @@
 KEYS = FR * 7 * COLS
 C = 384
 NEG = -1e30
+LIMIT = 62 << 20
+
+
+def lanes(ref):
+    return jnp.concatenate([ref[i : i + 1] for i in range(ref.shape[0])], axis=-1)
 
 
 def attend_kernel(
     n_rows,
-    stream_ref,
+    stream_hbm,
     q_ref,
     k_ref,
     v_ref,
-    mods_ref,
+    gate_hbm,
+    shift_hbm,
+    scale_hbm,
+    hw_hbm,
+    hb_hbm,
+    mean_hbm,
+    std_hbm,
+    cw_hbm,
+    cib_hbm,
+    gain_hbm,
+    cb_hbm,
+    w_hbm,
+    out_hbm,
+    w4_ref,
+    w_ref,
+    cib_ref,
+    gain_ref,
+    cb_ref,
+    stream_ref,
+    gate_ref,
+    shift_ref,
+    scale_ref,
     hw_ref,
-    small_ref,
-    out_ref,
+    hb_ref,
+    mean_ref,
+    std_ref,
+    cw_ref,
+    load_sem,
     qb,
     kb,
     vb,
@@ -47,6 +76,11 @@
     r3,
     s4,
     r4,
+    var,
+    acc,
+    wide,
+    done,
+    out_sem,
 ):
     row = lax.axis_index("row")
     g = row // GROUP
@@ -143,6 +177,27 @@
             device_id={"row": dev},
         )
 
+    pairs = (
+        (stream_hbm, stream_ref),
+        (gate_hbm, gate_ref),
+        (shift_hbm, shift_ref),
+        (scale_hbm, scale_ref),
+        (hw_hbm, hw_ref),
+        (hb_hbm, hb_ref),
+        (mean_hbm, mean_ref),
+        (std_hbm, std_ref),
+        (cw_hbm, cw_ref),
+        (cib_hbm, cib_ref),
+        (gain_hbm, gain_ref),
+        (cb_hbm, cb_ref),
+        (w_hbm, w_ref),
+    )
+    loads = [
+        pltpu.make_async_copy(src, dst, load_sem.at[i]) for i, (src, dst) in enumerate(pairs)
+    ]
+    for cp in loads:
+        cp.start()
+
     tok_i = lax.broadcasted_iota(jnp.int32, (TOK, KEYS), 0)
     key_i = lax.broadcasted_iota(jnp.int32, (TOK, KEYS), 1)
     t = tok_i >> 5
@@ -181,6 +236,13 @@
 
     for cp in own:
         cp.wait()
+    for cp in loads[:-1]:
+        cp.wait()
+
+    w4_ref[...] = jnp.zeros(w4_ref.shape, jnp.bfloat16)
+    for ab in range(9):
+        w4_ref[ab * 64 : ab * 64 + 48, 0:C] = cw_ref[ab]
+        w4_ref[ab * 64 + 16 : ab * 64 + 64, C : 2 * C] = cw_ref[ab]
 
     for h in range(HPD):
         for x in range(2):
@@ -254,15 +316,20 @@
             out_copy(h, d).wait_recv()
 
     attn_all = jnp.concatenate([attn[c] for c in range(HEADS)], axis=-1)
-    resid = stream_ref[...].astype(jnp.float32) + mods_ref[0:1, :] * attn_all.astype(jnp.float32)
+    resid = stream_ref[...].astype(jnp.float32) + lanes(gate_ref) * attn_all.astype(jnp.float32)
     center = resid - jnp.mean(resid, axis=-1, keepdims=True)
     spread = jnp.mean(center * center, axis=-1, keepdims=True)
-    normed = center * lax.rsqrt(spread + 1e-06) * (1.0 + mods_ref[2:3, :]) + mods_ref[1:2, :]
-    patch = jnp.dot(
-        normed.astype(jnp.bfloat16), hw_ref[...], preferred_element_type=jnp.float32
-    )
-    patch = patch + small_ref[0:1, :]
-    latent = (patch * small_ref[1:2, :] + small_ref[2:3, :]).astype(jnp.bfloat16)
+    normed = center * lax.rsqrt(spread + 1e-06) * (1.0 + lanes(scale_ref)) + lanes(shift_ref)
+    patch = lax.dot_general(
+        normed.astype(jnp.bfloat16),
+        hw_ref[...],
+        (((1,), (1,)), ((), ())),
+        preferred_element_type=jnp.float32,
+    )
+    patch = patch + hb_ref[...]
+    std = jnp.concatenate([std_ref[...]] * 4, axis=-1)
+    mean = jnp.concatenate([mean_ref[...]] * 4, axis=-1)
+    latent = (patch * std + mean).astype(jnp.bfloat16)
 
     dst_l = lax.broadcasted_iota(jnp.int32, (4 * LAT, 128), 1)
     src_l = lax.broadcasted_iota(jnp.int32, (4 * LAT, 128), 0)
@@ -323,74 +390,73 @@
         latent_copy(False).wait_send()
         latent_copy(True).wait_recv()
 
-    out_ref[...] = gbuf[...]
-
-
-def decode_kernel(n_rows, cells_ref, cw_ref, vec_ref, w_ref, out_ref, w4, var, acc, wide):
-    step = pl.program_id(0)
-    a = step // 3
-    b = step % 3
-
-    @pl.when(step == 0)
-    def _():
-        row = lax.axis_index("row")
-        w4[...] = jnp.zeros(w4.shape, jnp.bfloat16)
-        for ab in range(9):
-            w4[ab * 64 : ab * 64 + 48, 0:C] = cw_ref[ab]
-            w4[ab * 64 + 16 : ab * 64 + 64, C : 2 * C] = cw_ref[ab]
-        six = jnp.concatenate([cells_ref[i] for i in range(3)], axis=-1)
-        col = lax.broadcasted_iota(jnp.int32, (TOK, C), 0) & 31
-        zeros = jnp.zeros((2 * COLS, C), jnp.bfloat16)
-        pad = jnp.zeros((2 * COLS, 192), jnp.bfloat16)
-        for y in range(4):
-            rows3 = six[:, y * 64 : y * 64 + 192]
-            padded = jnp.concatenate([pad, rows3], axis=0)
-            x = jnp.concatenate(
-                [padded[i * COLS : i * COLS + TOK] for i in range(3)], axis=-1
-            )
-            h = jnp.dot(x, w4[...], preferred_element_type=jnp.float32)
-            acts = []
-            for q in range(2):
-                hidden = (h[:, q * C : (q + 1) * C] + vec_ref[0:1, :]).astype(jnp.bfloat16)
-                hidden = hidden.astype(jnp.float32)
-                if y in (1, 2):
-                    at = ((y - 1) * 2 + q) * TOK
-                    acc[at : at + TOK, :] = hidden + vec_ref[2:3, :]
-                ms = jnp.mean(hidden * hidden, axis=-1, keepdims=True)
-                scaled = hidden * lax.rsqrt(ms + 1e-06) * vec_ref[1:2, :]
-                act = scaled / (1.0 + jnp.exp(-scaled))
-                if y == 0:
-                    act = jnp.where(row > 0, act, 0.0)
-                if y == 3:
-                    act = jnp.where(row < n_rows - 1, act, 0.0)
-                acts.append(act)
-            before = jnp.where(col == 0, 0.0, pltpu.roll(acts[1], 1, 0))
-            after = jnp.where(col == COLS - 1, 0.0, pltpu.roll(acts[0], TOK - 1, 0))
-            for i, piece in enumerate((before, acts[0], acts[1], after)):
-                var[i, y, 0 : 2 * COLS] = zeros
-                var[i, y, 2 * COLS :] = piece.astype(jnp.bfloat16)
-
-    start = pl.multiple_of(a * COLS, COLS)
-    phases = []
-    for y in range(2):
-        taps = [var[i, y + b, pl.ds(start, TOK)] for i in range(4)]
+    loads[-1].wait()
+    decode(
+        row, n_rows, gbuf, w4_ref, w_ref, cib_ref, gain_ref, cb_ref, out_hbm, var, acc, wide, done,
+        out_sem,
+    )
+
+
+def decode(
+    row, n_rows, cells_ref, w4_ref, w_ref, cib_ref, gain_ref, cb_ref, out_hbm, var, acc, wide, done,
+    sem,
+):
+    six = jnp.concatenate([cells_ref[i] for i in range(3)], axis=-1)
+    col = lax.broadcasted_iota(jnp.int32, (TOK, C), 0) & 31
+    zeros = jnp.zeros((2 * COLS, C), jnp.bfloat16)
+    pad = jnp.zeros((2 * COLS, 192), jnp.bfloat16)
+    for y in range(4):
+        rows3 = six[:, y * 64 : y * 64 + 192]
+        padded = jnp.concatenate([pad, rows3], axis=0)
+        x = jnp.concatenate([padded[i * COLS : i * COLS + TOK] for i in range(3)], axis=-1)
+        h = jnp.dot(x, w4_ref[...], preferred_element_type=jnp.float32)
+        acts = []
         for q in range(2):
-            phases.append(jnp.concatenate(taps[q : q + 3], axis=-1))
-    lhs = jnp.concatenate(phases, axis=0)
-    acc[...] += jnp.dot(lhs, w_ref[0], preferred_element_type=jnp.float32)
-
-    @pl.when(step == 8)
-    def _():
+            hidden = (h[:, q * C : (q + 1) * C] + lanes(cib_ref)).astype(jnp.bfloat16)
+            hidden = hidden.astype(jnp.float32)
+            if y in (1, 2):
+                at = ((y - 1) * 2 + q) * TOK
+                acc[at : at + TOK, :] = hidden + lanes(cb_ref)
+            ms = jnp.mean(hidden * hidden, axis=-1, keepdims=True)
+            scaled = hidden * lax.rsqrt(ms + 1e-06) * lanes(gain_ref)
+            act = scaled / (1.0 + jnp.exp(-scaled))
+            if y == 0:
+                act = jnp.where(row > 0, act, 0.0)
+            if y == 3:
+                act = jnp.where(row < n_rows - 1, act, 0.0)
+            acts.append(act)
+        before = jnp.where(col == 0, 0.0, pltpu.roll(acts[1], 1, 0))
+        after = jnp.where(col == COLS - 1, 0.0, pltpu.roll(acts[0], TOK - 1, 0))
+        for i, piece in enumerate((before, acts[0], acts[1], after)):
+            var[i, y, 0 : 2 * COLS] = zeros
+            var[i, y, 2 * COLS :] = piece.astype(jnp.bfloat16)
+
+    for a in range(3):
+        for b in range(3):
+            phases = []
+            for y in range(2):
+                taps = [var[i, y + b, a * COLS : a * COLS + TOK] for i in range(4)]
+                for q in range(2):
+                    phases.append(jnp.concatenate(taps[q : q + 3], axis=-1))
+            lhs = jnp.concatenate(phases, axis=0)
+            acc[...] += jnp.dot(lhs, w_ref[a * 3 + b], preferred_element_type=jnp.float32)
+
+    copies = []
+    for t in range(FR):
         for y in range(2):
             for q in range(2):
-                for t in range(FR):
-                    at = (y * 2 + q) * TOK + t * COLS
-                    for c in range(3):
-                        wide[t, y, c, pl.ds(q, COLS, stride=2), :] = acc[
-                            at : at + COLS, c * 128 : (c + 1) * 128
-                        ]
+                at = (y * 2 + q) * TOK + t * COLS
+                for c in range(3):
+                    wide[t, y, c, pl.ds(q, COLS, stride=2), :] = acc[
+                        at : at + COLS, c * 128 : (c + 1) * 128
+                    ]
         for c in range(3):
-            out_ref[:, :, :, c * 128 : (c + 1) * 128] = wide[:, :, c].astype(jnp.bfloat16)
+            done[t, :, :, c * 128 : (c + 1) * 128] = wide[t, :, c].astype(jnp.bfloat16)
+        cp = pltpu.make_async_copy(done.at[t], out_hbm.at[t], sem.at[t])
+        cp.start()
+        copies.append(cp)
+    for cp in copies:
+        cp.wait()
 
 
 def shards(
@@ -414,25 +480,39 @@
 ):
     width = query.shape[-1]
     flat = (FR, COLS, width)
-    mods = jnp.stack([attn_gate, shift_mod, scale_mod])
-    small = jnp.stack([head_bias, jnp.tile(latent_std, 4), jnp.tile(latent_mean, 4)])
-    vecs = jnp.stack([conv_in_bias, norm_gain, conv_bias])
-    vmem = pl.BlockSpec(memory_space=pltpu.VMEM)
-    anywhere = pl.BlockSpec(memory_space=pl.ANY)
+    hbm = pl.BlockSpec(memory_space=pltpu.HBM)
     dma = pltpu.SemaphoreType.DMA
     bf = jnp.bfloat16
-    cells = pl.pallas_call(
+    f32 = jnp.float32
+    line = lambda x: x.reshape(-1, min(128, x.shape[0]))
+    shape = jax.ShapeDtypeStruct
+    return pl.pallas_call(
         functools.partial(attend_kernel, n_rows),
-        out_shape=jax.ShapeDtypeStruct((3, TOK, 128), bf),
-        in_specs=[vmem, anywhere, anywhere, anywhere, vmem, vmem, vmem],
-        out_specs=vmem,
+        out_shape=shape((FR, 2, 2 * COLS, C), bf),
+        in_specs=[hbm] * 16,
+        out_specs=hbm,
         scratch_shapes=[
+            pltpu.VMEM((576, 2 * C), bf),
+            pltpu.VMEM((9, 3 * C, C), bf),
+            pltpu.VMEM((C // 128, 128), f32),
+            pltpu.VMEM((C // 128, 128), f32),
+            pltpu.VMEM((C // 128, 128), f32),
+            pltpu.VMEM((TOK, width), bf),
+            pltpu.VMEM((width // 128, 128), f32),
+            pltpu.VMEM((width // 128, 128), f32),
+            pltpu.VMEM((width // 128, 128), f32),
+            pltpu.VMEM((4 * LAT, width), bf),
+            pltpu.VMEM((1, 4 * LAT), f32),
+            pltpu.VMEM((1, LAT), f32),
+            pltpu.VMEM((1, LAT), f32),
+            pltpu.VMEM((9, 3 * LAT, C), bf),
+            dma((13,)),
             pltpu.VMEM((HPD, GROUP, FR, COLS, HD), bf),
             pltpu.VMEM((HPD, FR, ROWS_EXT, COLS, HD), bf),
             pltpu.VMEM((HPD, FR, ROWS_EXT, COLS, HD), bf),
             pltpu.VMEM((HPD, GROUP, TOK, HD), bf),
             pltpu.VMEM((HEADS, TOK, HD), bf),
-            pltpu.VMEM((TOK, KEYS), jnp.float32),
+            pltpu.VMEM((TOK, KEYS), f32),
             pltpu.VMEM((3, TOK, 128), bf),
             dma((3, HPD)),
             dma((3, HPD, 3)),
@@ -443,9 +523,14 @@
             dma((HPD, 3)),
             dma((2,)),
             dma((2,)),
+            pltpu.VMEM((4, 4, 2 * COLS + TOK, C), bf),
+            pltpu.VMEM((4 * TOK, C), f32),
+            pltpu.VMEM((FR, 2, 3, 2 * COLS, 128), f32),
+            pltpu.VMEM((FR, 2, 2 * COLS, C), bf),
+            dma((FR,)),
         ],
         compiler_params=pltpu.CompilerParams(
-            collective_id=0, has_side_effects=True, vmem_limit_bytes=24 << 20
+            collective_id=0, has_side_effects=True, vmem_limit_bytes=LIMIT
         ),
         name="attend",
     )(
@@ -453,34 +538,17 @@
         query.reshape(flat),
         key.reshape(flat),
         value.reshape(flat),
-        mods,
-        head_weight,
-        small,
-    )
-    whole = lambda *shape: pl.BlockSpec(shape, lambda s: (0,) * len(shape))
-    return pl.pallas_call(
-        functools.partial(decode_kernel, n_rows),
-        out_shape=jax.ShapeDtypeStruct((FR, 2, 2 * COLS, C), bf),
-        grid=(9,),
-        in_specs=[
-            whole(3, TOK, 128),
-            whole(9, 3 * LAT, C),
-            whole(3, C),
-            pl.BlockSpec((1, 3 * C, C), lambda s: (s, 0, 0)),
-        ],
-        out_specs=whole(FR, 2, 2 * COLS, C),
-        scratch_shapes=[
-            pltpu.VMEM((576, 2 * C), bf),
-            pltpu.VMEM((4, 4, 2 * COLS + TOK, C), bf),
-            pltpu.VMEM((4 * TOK, C), jnp.float32),
-            pltpu.VMEM((FR, 2, 3, 2 * COLS, 128), jnp.float32),
-        ],
-        compiler_params=pltpu.CompilerParams(vmem_limit_bytes=32 << 20),
-        name="decode",
-    )(
-        cells,
+        line(attn_gate),
+        line(shift_mod),
+        line(scale_mod),
+        head_weight.T,
+        line(head_bias),
+        line(latent_mean),
+        line(latent_std),
         conv_in_weight.reshape(9, 3 * LAT, C),
-        vecs,
+        line(conv_in_bias),
+        line(norm_gain),
+        line(conv_bias),
         conv_weight.reshape(9, 3 * C, C),
     )
 

time: 57.9 us -> 41.9 us (0.72)
  local copies, waits for them, and re-layouts: 15 us -> 1.78 us
  Pallas kernels: 41.6 us -> 39.9 us
  other arithmetic: 0.7 us -> 0 us
    unnamed x13 -> x1, local copies, waits for them, and re-layouts: 9.36 us -> 1.78 us
    another operation x10 -> x0, local copies, waits for them, and re-layouts: 5.64 us -> none  [the longest x3 2.11 us: shards(): mods = jnp.stack([attn_gate, shift_mod, scale_mod])]
    pallas_call x2 -> x1, Pallas kernels: 41.6 us -> 39.9 us  [shards(): pl.pallas_call(functools.partial(attend_kernel, n_rows), out_shape=shape(...]
    another operation x3 -> x0, other arithmetic: 0.7 us -> none  [the longest x1 0.67 us: shards(): jnp.stack([head_bias, jnp.tile(latent_std, 4), jnp.tile(latent_mean, 4)])]
where the time goes in v2:
time: 41.9 us; the launch traced here: 41.7 us
  Pallas kernels  39.9 us (95%)
  local copies, waits for them, and re-layouts  1.78 us (4%)
    pallas_call x1, Pallas kernels, shards(): pl.pallas_call(functools.partial(attend_kernel, n_rows), out_shape=shape(...  39.9 us
    unnamed x1, local copies, waits for them, and re-layouts  1.78 us

profile of v2, /device:TPU:1, one launch (start us, length us, event | category | flops | bytes accessed | tf_op | source)
XLA Modules:
  0.0 41.7 jit_solution(7293624183145916579)
XLA Ops:
  0.0 39.9 %attend.1 = bf16[4,2,64,384]{3,2,1,0:T(8,128)(2,1)} custom-call(bf16[128,1536]{1,0:T(8,128)(2,1)} %bitcast.17, bf16[4,32,1536]{2,1,0:T(8,128)(2,1)} %bitcast.18, bf16[4,32,1536]{2,1,0:T(8,128)(2,1)} %bitcast.19, bf16[4,32,1536]{2,1,0:T(8,128)(2,1)} %bitcast.20, f32[12,128]{1,0:T(8,128)} %bitcast.23, f32[12,128]{1,0:T(8,128)} %bitcast.24, ...), custom_call_target="tpu_custom_call" | custom-call | tf_op jit(solution)/shard_map/attend/pallas_call | solution.py:489
  39.9 1.8 %copy.18 = bf16[4,2,64,384]{3,2,1,0:T(8,128)(2,1)} copy(bf16[4,2,64,384]{3,2,1,0:T(8,128)(2,1)} %attend.1) | data formatting | bytes 786432

commit v3 on v2

--- a/solution.py
+++ b/solution.py
@@ -72,6 +72,8 @@
     r1,
     s2,
     r2,
+    s5,
+    r5,
     s3,
     r3,
     s4,
@@ -86,6 +88,8 @@
     g = row // GROUP
     j = row % GROUP
     groups = n_rows // GROUP
+    half = j // 2
+    mate = j + 1 - 2 * (j % 2)
     has_up = g > 0
     has_down = g < groups - 1
     first = row == 0
@@ -116,11 +120,13 @@
 
     @pl.when(has_up)
     def _():
-        pl.semaphore_signal(barrier, inc=1, device_id={"row": row - GROUP})
+        for p in (j, mate):
+            pl.semaphore_signal(barrier, inc=1, device_id={"row": (g - 1) * GROUP + p})
 
     @pl.when(has_down)
     def _():
-        pl.semaphore_signal(barrier, inc=1, device_id={"row": row + GROUP})
+        for p in (j, mate):
+            pl.semaphore_signal(barrier, inc=1, device_id={"row": (g + 1) * GROUP + p})
 
     cross_up = jnp.logical_and(j == 0, has_up)
     cross_down = jnp.logical_and(j == GROUP - 1, has_down)
@@ -137,8 +143,8 @@
     zero = jnp.int32(0)
     expected = (
         3
-        + jnp.where(has_up, one, zero)
-        + jnp.where(has_down, one, zero)
+        + 2 * jnp.where(has_up, one, zero)
+        + 2 * jnp.where(has_down, one, zero)
         + jnp.where(cross_up, one, zero)
         + jnp.where(cross_down, one, zero)
     )
@@ -154,21 +160,15 @@
             device_id={"row": g * GROUP + p},
         )
 
-    for h in range(HPD):
-        for x in range(2):
-            for d in (2, 1, 3):
-                level_copy(x, h, d).start()
-    for h in range(HPD):
-        for d in (2, 1, 3):
-            level_copy(2, h, d).start()
-
-    def edge_copy(x, h, up):
+    def relay_copy(x, h, two):
         buf = (kb, vb)[x]
-        if up:
-            src, dst, dev = buf.at[h, :, pl.ds(3, 3)], buf.at[h, :, pl.ds(7, 3)], row - GROUP
+        if two:
+            src, dst = buf.at[h, :, pl.ds(5 - 2 * half, 2)], buf.at[h, :, pl.ds(1 + 6 * half, 2)]
+            dev = row + GROUP - 2 * GROUP * half
         else:
-            src, dst, dev = buf.at[h, :, pl.ds(4, 3)], buf.at[h, :, pl.ds(0, 3)], row + GROUP
-        way = 0 if up else 1
+            src, dst = buf.at[h, :, pl.ds(5 - half, 1)], buf.at[h, :, pl.ds(9 - 9 * half, 1)]
+            dev = row - GROUP + 2 * GROUP * half
+        way = 0 if two else 1
         return pltpu.make_async_remote_copy(
             src_ref=src,
             dst_ref=dst,
@@ -176,6 +176,50 @@
             recv_sem=r2.at[x, h, way],
             device_id={"row": dev},
         )
+
+    ahead = jnp.logical_or(
+        jnp.logical_and(half == 0, has_down), jnp.logical_and(half == 1, has_up)
+    )
+    behind = jnp.logical_or(
+        jnp.logical_and(half == 0, has_up), jnp.logical_and(half == 1, has_down)
+    )
+
+    def straight_copy(x, h, up, c, at):
+        p = (j, mate)[c]
+        way = 0 if up else 1
+        return pltpu.make_async_remote_copy(
+            src_ref=srcs[x].at[:, :, head_cols(p, h)],
+            dst_ref=(kb, vb)[x].at[h, :, at],
+            send_sem=s5.at[x, h, way, c],
+            recv_sem=r5.at[x, h, way, c],
+            device_id={"row": (g - 1 if up else g + 1) * GROUP + p},
+        )
+
+    send_up = jnp.logical_and(has_up, j <= 2)
+    send_down = jnp.logical_and(has_down, j >= 1)
+    recv_up = [jnp.logical_and(has_down, p <= 2) for p in (j, mate)]
+    recv_down = [jnp.logical_and(has_up, p >= 1) for p in (j, mate)]
+
+    for h in range(HPD):
+        for x in range(2):
+            for d in (2, 1, 3):
+                level_copy(x, h, d).start()
+
+        @pl.when(send_up)
+        def _():
+            for x in range(2):
+                for c in range(2):
+                    straight_copy(x, h, True, c, 7 + j).start()
+
+        @pl.when(send_down)
+        def _():
+            for x in range(2):
+                for c in range(2):
+                    straight_copy(x, h, False, c, j - 1).start()
+
+    for h in range(HPD):
+        for d in (2, 1, 3):
+            level_copy(2, h, d).start()
 
     pairs = (
         (stream_hbm, stream_ref),
@@ -249,13 +293,13 @@
             for d in range(1, GROUP):
                 level_copy(x, h, d).wait_recv()
 
-            @pl.when(has_up)
-            def _():
-                edge_copy(x, h, True).start()
-
-            @pl.when(has_down)
-            def _():
-                edge_copy(x, h, False).start()
+            @pl.when(ahead)
+            def _():
+                relay_copy(x, h, True).start()
+
+            @pl.when(behind)
+            def _():
+                relay_copy(x, h, False).start()
 
     key_row = lax.broadcasted_iota(jnp.int32, (1, KEYS), 1)
     fr = (
@@ -280,15 +324,25 @@
             level_copy(2, h, d).wait_recv()
         for x in range(2):
 
-            @pl.when(has_down)
-            def _():
-                edge_copy(x, h, True).wait_recv()
-
-            @pl.when(has_up)
-            def _():
-                edge_copy(x, h, False).wait_recv()
-
-        def one_row(i, carry):
+            @pl.when(behind)
+            def _():
+                relay_copy(x, h, True).wait_recv()
+
+            @pl.when(ahead)
+            def _():
+                relay_copy(x, h, False).wait_recv()
+
+            for c in range(2):
+
+                @pl.when(recv_up[c])
+                def _():
+                    straight_copy(x, h, True, c, 7).wait_recv()
+
+                @pl.when(recv_down[c])
+                def _():
+                    straight_copy(x, h, False, c, 0).wait_recv()
+
+        def one_row(i):
             qm = qb[h, i].reshape(TOK, HD)
             km = kb[h, :, pl.ds(i, 7)].reshape(KEYS, HD)
             vm = vb[h, :, pl.ds(i, 7)].reshape(KEYS, HD)
@@ -303,13 +357,13 @@
             l = jnp.sum(e, axis=1, keepdims=True)
             pr = (e * (1.0 / l)).astype(jnp.bfloat16)
             o = jnp.dot(pr, vm, preferred_element_type=jnp.float32)
-            ob[h, i] = o.astype(jnp.bfloat16)
-            return carry
-
-        lax.fori_loop(0, GROUP, one_row, 0)
+            return o.astype(jnp.bfloat16)
+
         for d in (2, 1, 3):
+            i = (j + d) % GROUP
+            ob[h, i] = one_row(i)
             out_copy(h, d).start()
-        attn[j * HPD + h] = ob[h, j]
+        attn[j * HPD + h] = one_row(j)
 
     for h in range(HPD):
         for d in range(1, GROUP):
@@ -369,13 +423,23 @@
                 level_copy(x, h, d).wait_send()
         for x in range(2):
 
-            @pl.when(has_up)
-            def _():
-                edge_copy(x, h, True).wait_send()
-
-            @pl.when(has_down)
-            def _():
-                edge_copy(x, h, False).wait_send()
+            @pl.when(ahead)
+            def _():
+                relay_copy(x, h, True).wait_send()
+
+            @pl.when(behind)
+            def _():
+                relay_copy(x, h, False).wait_send()
+
+            @pl.when(send_up)
+            def _():
+                for c in range(2):
+                    straight_copy(x, h, True, c, 7).wait_send()
+
+            @pl.when(send_down)
+            def _():
+                for c in range(2):
+                    straight_copy(x, h, False, c, 0).wait_send()
 
         for d in range(1, GROUP):
             out_copy(h, d).wait_send()
@@ -519,6 +583,8 @@
             dma((3, HPD, 3)),
             dma((2, HPD, 2)),
             dma((2, HPD, 2)),
+            dma((2, HPD, 2, 2)),
+            dma((2, HPD, 2, 2)),
             dma((HPD, 3)),
             dma((HPD, 3)),
             dma((2,)),

time: 41.9 us -> 39.2 us (0.936)
  Pallas kernels: 39.9 us -> 37.2 us
    pallas_call x1, Pallas kernels: 39.9 us -> 37.2 us  [shards(): pl.pallas_call(functools.partial(attend_kernel, n_rows), out_shape=shape(...]
where the time goes in v3:
time: 39.2 us; the launch traced here: 39 us
  Pallas kernels  37.2 us (95%)
  local copies, waits for them, and re-layouts  1.78 us (5%)
    pallas_call x1, Pallas kernels, shards(): pl.pallas_call(functools.partial(attend_kernel, n_rows), out_shape=shape(...  37.2 us
    unnamed x1, local copies, waits for them, and re-layouts  1.78 us

profile of v3, /device:TPU:1, one launch (start us, length us, event | category | flops | bytes accessed | tf_op | source)
XLA Modules:
  0.0 39.0 jit_solution(7843541795776464332)
XLA Ops:
  0.0 37.2 %attend.1 = bf16[4,2,64,384]{3,2,1,0:T(8,128)(2,1)} custom-call(bf16[128,1536]{1,0:T(8,128)(2,1)} %bitcast.17, bf16[4,32,1536]{2,1,0:T(8,128)(2,1)} %bitcast.18, bf16[4,32,1536]{2,1,0:T(8,128)(2,1)} %bitcast.19, bf16[4,32,1536]{2,1,0:T(8,128)(2,1)} %bitcast.20, f32[12,128]{1,0:T(8,128)} %bitcast.23, f32[12,128]{1,0:T(8,128)} %bitcast.24, ...), custom_call_target="tpu_custom_call" | custom-call | tf_op jit(solution)/shard_map/attend/pallas_call | solution.py:553
  37.2 1.8 %copy.18 = bf16[4,2,64,384]{3,2,1,0:T(8,128)(2,1)} copy(bf16[4,2,64,384]{3,2,1,0:T(8,128)(2,1)} %attend.1) | data formatting | bytes 786432

commit v4 on v3

--- a/solution.py
+++ b/solution.py
@@ -280,6 +280,20 @@
 
     for cp in own:
         cp.wait()
+
+    for h in range(HPD):
+        for x in range(2):
+            for d in range(1, GROUP):
+                level_copy(x, h, d).wait_recv()
+
+            @pl.when(ahead)
+            def _():
+                relay_copy(x, h, True).start()
+
+            @pl.when(behind)
+            def _():
+                relay_copy(x, h, False).start()
+
     for cp in loads[:-1]:
         cp.wait()
 
@@ -287,19 +301,6 @@
     for ab in range(9):
         w4_ref[ab * 64 : ab * 64 + 48, 0:C] = cw_ref[ab]
         w4_ref[ab * 64 + 16 : ab * 64 + 64, C : 2 * C] = cw_ref[ab]
-
-    for h in range(HPD):
-        for x in range(2):
-            for d in range(1, GROUP):
-                level_copy(x, h, d).wait_recv()
-
-            @pl.when(ahead)
-            def _():
-                relay_copy(x, h, True).start()
-
-            @pl.when(behind)
-            def _():
-                relay_copy(x, h, False).start()
 
     key_row = lax.broadcasted_iota(jnp.int32, (1, KEYS), 1)
     fr = (

time: 39.2 us -> 39.2 us (level)
  no operation moved by 1% of the time
where the time goes in v4:
time: 39.2 us; the launch traced here: 39 us
  Pallas kernels  37.2 us (95%)
  local copies, waits for them, and re-layouts  1.78 us (5%)
    pallas_call x1, Pallas kernels, shards(): pl.pallas_call(functools.partial(attend_kernel, n_rows), out_shape=shape(...  37.2 us
    unnamed x1, local copies, waits for them, and re-layouts  1.78 us

profile of v4, /device:TPU:1, one launch (start us, length us, event | category | flops | bytes accessed | tf_op | source)
XLA Modules:
  0.0 39.0 jit_solution(6790336849176144021)
XLA Ops:
  0.0 37.2 %attend.1 = bf16[4,2,64,384]{3,2,1,0:T(8,128)(2,1)} custom-call(bf16[128,1536]{1,0:T(8,128)(2,1)} %bitcast.17, bf16[4,32,1536]{2,1,0:T(8,128)(2,1)} %bitcast.18, bf16[4,32,1536]{2,1,0:T(8,128)(2,1)} %bitcast.19, bf16[4,32,1536]{2,1,0:T(8,128)(2,1)} %bitcast.20, f32[12,128]{1,0:T(8,128)} %bitcast.23, f32[12,128]{1,0:T(8,128)} %bitcast.24, ...), custom_call_target="tpu_custom_call" | custom-call | tf_op jit(solution)/shard_map/attend/pallas_call | solution.py:554
  37.2 1.8 %copy.18 = bf16[4,2,64,384]{3,2,1,0:T(8,128)(2,1)} copy(bf16[4,2,64,384]{3,2,1,0:T(8,128)(2,1)} %attend.1) | data formatting | bytes 786432
